TPU v7x, 32 devices: a whole 2x2x4 slice. The times are simulated.
32 devices in a mesh: stn: 2 (over x), vox: 16 (over z, y, core).
Axes of the slice: x: 2, y: 2, z: 4, core: 2. Of those that a mesh axis runs over, the one named last changes fastest.
Arguments:
- voltages: bfloat16 [56, 2, 65536], P('stn', None, 'vox'), may hold values from -6 to 6
- sample_delays: int32 [56, 65536], P(None, 'vox'), may hold values from 0 to 239
- timing_offsets: int32 [56], replicated, may hold values from 0 to 15
- reference_station: int32 [1], replicated, may hold values from 0 to 55
Outputs:
- image_out: float32 [64, 65536], P('stn', 'vox')
All inputs are finite; a program needn't handle non-finite values.
Results may differ from a plain program's by a relative error of at most 0.004.
Values may be sent and summed in bfloat16 or wider, within the bound.
No kernel may reach another device: no remote copies, remote signals or barrier semaphores. Data moves between devices by JAX's collectives and lax.ppermute only.
A program may use at most 64 MiB of HBM per device.

v0:
```python
import math
import jax
import jax.numpy as jnp
from jax import lax
from jax.sharding import PartitionSpec as P

STATIONS = 56
WIN = 1024
LAGS = 256


def spread(value, axis, source):
    kept = jnp.where(lax.axis_index(axis) == source, value, 0).astype(value.dtype)
    return lax.psum(kept, axis)


def padded(block, sides, width):
    for axis, dim in sides:
        count = lax.axis_size(axis)
        forward = [(i, i + 1) for i in range(count - 1)]
        backward = [(target, source) for source, target in forward]
        low = lax.ppermute(
            lax.slice_in_dim(block, block.shape[dim] - width, None, axis=dim), axis, forward
        )
        high = lax.ppermute(lax.slice_in_dim(block, 0, width, axis=dim), axis, backward)
        block = jnp.concatenate([low, block, high], axis=dim)
    return block


def taper_weights(length):
    position = (jnp.arange(length, dtype=jnp.float32) + 0.5) / length
    return 0.5 - 0.5 * jnp.cos(2.0 * math.pi * position)


def shards(voltages, sample_delays, timing_offsets, reference_station):
    stations_here, polarizations, samples_here = voltages.shape
    slices_here = samples_here // WIN
    voxels_here = sample_delays.shape[1]
    station_ref = reference_station[0]
    stn_index = lax.axis_index("stn")
    taper_curve = taper_weights(WIN)
    norm_inv = 1.0 / jnp.sqrt(jnp.sum(taper_curve * taper_curve))
    owner_index = station_ref // stations_here
    ref_local = lax.dynamic_index_in_dim(voltages, station_ref % stations_here, 0, keepdims=False)
    ref_signal = spread(ref_local, "stn", owner_index)
    extended = padded(ref_signal, (("vox", 1),), LAGS // 2)
    extended = jnp.pad(extended, ((0, 0), (0, WIN)))
    leading = extended[:, :samples_here].reshape(polarizations, slices_here, WIN)
    trailing = extended[:, WIN : samples_here + WIN].reshape(polarizations, slices_here, WIN)[
        :, :, : LAGS - 1
    ]
    segments = jnp.concatenate([leading, trailing], axis=2).reshape(
        1, polarizations * slices_here, WIN + LAGS - 1
    )
    windowed = (
        voltages.reshape(stations_here, polarizations, slices_here, WIN) * taper_curve
    ).astype(jnp.bfloat16)
    kernels = jnp.transpose(windowed, (1, 2, 0, 3)).reshape(
        polarizations * slices_here * stations_here, 1, WIN
    )
    lagged_sums = lax.conv_general_dilated(
        segments,
        kernels,
        (1,),
        "VALID",
        feature_group_count=polarizations * slices_here,
        preferred_element_type=jnp.float32,
    )
    lagged_sums = jnp.sum(
        lagged_sums.reshape(polarizations, slices_here, stations_here, LAGS), axis=0
    )
    station_ids = stn_index * stations_here + jnp.arange(stations_here, dtype=jnp.int32)
    keep_mask = (station_ids != station_ref).astype(jnp.float32)
    local_corr = (
        jnp.transpose(lagged_sums, (1, 0, 2)) * keep_mask[:, None, None] * norm_inv
    ).astype(jnp.bfloat16)
    corr_all = lax.all_gather(local_corr, "vox", axis=1, tiled=True)
    lag_index = sample_delays + timing_offsets[:, None]
    total_slices = corr_all.shape[1]
    out_scale = 1.0 / math.sqrt(2.0 * STATIONS)
    my_lags = lax.dynamic_slice_in_dim(lag_index, stn_index * stations_here, stations_here, 0)
    corr_block = lax.slice_in_dim(
        corr_all, 0, lax.axis_size("stn") * (total_slices // lax.axis_size("stn")), axis=1
    )
    lag_grid = lax.broadcasted_iota(jnp.int32, (LAGS, voxels_here), 0)

    def add_station(running, inputs_pair):
        corr_rows, lags_one = inputs_pair
        selector = (lag_grid == lags_one[None, :]).astype(jnp.bfloat16)
        return (running + jnp.dot(corr_rows, selector, preferred_element_type=jnp.float32), None)

    running, unused = lax.scan(
        add_station,
        jnp.zeros(
            (lax.axis_size("stn") * (total_slices // lax.axis_size("stn")), voxels_here),
            jnp.float32,
        ),
        (corr_block, my_lags),
    )
    image_out = lax.psum_scatter(running, "stn", scatter_dimension=0, tiled=True)
    return image_out * out_scale


def solution(mesh):
    return jax.shard_map(
        shards,
        mesh=mesh,
        in_specs=(P("stn", None, "vox"), P(None, "vox"), P(), P()),
        out_specs=P("stn", "vox"),
        check_vma=False,
    )
```

profile of v0, /device:TPU:0, one launch (start us, length us, event | category | flops | bytes accessed | tf_op | source)
XLA Modules:
  0.0 126.3 jit_solution(5938789996437528588)
XLA Ops:
  6.5 0.0 reduce-scatter.2.cloned.1.call-start
  7.2 0.7 fusion.14
  8.0 9.7 %psum.7 = bf16[2,4096]{1,0:T(2,128)(2,1)S(1)} all-reduce(bf16[2,4096]{1,0:T(2,128)(2,1)S(1)} %fusion.14), channel_id=1, replica_groups=mesh['stn'=2,'vox'=16] {'stn'}, use_global_device_ids=true, to_apply=%region_0.0 | all-reduce | flops 8192 | bytes 32768 | tf_op jit(solution)/shard_map/psum | solution.py:14
  17.6 1.3 %collective-permute-start = (bf16[2,128]{1,0:T(2,128)(2,1)S(1)}, bf16[2,128]{1,0:T(2,128)(2,1)S(1)}, u32[]{:S(2)}, u32[]{:S(2)}) collective-permute-start(bf16[2,128]{1,0:T(2,128)(2,1)S(1)} %get-tuple-element.64), channel_id=1, source_target_pairs={{0,1},{1,2},{2,3},{3,4},{4,5},{5,6},{6,7},{7,8},{8,9},{9,10},{10,1... | collective-permute-start | bytes 1544 | tf_op jit(solution)/shard_map/ppermute | solution.py:22
  18.9 1.3 %collective-permute-start.1 = (bf16[2,128]{1,0:T(2,128)(2,1)S(1)}, bf16[2,128]{1,0:T(2,128)(2,1)S(1)}, u32[]{:S(2)}, u32[]{:S(2)}) collective-permute-start(bf16[2,128]{1,0:T(2,128)(2,1)S(1)} %get-tuple-element.65), channel_id=1, source_target_pairs={{1,0},{2,1},{3,2},{4,3},{5,4},{6,5},{7,6},{8,7},{9,8},{10,9},{11,1... | collective-permute-start | bytes 1544 | tf_op jit(solution)/shard_map/ppermute | solution.py:25
  20.2 1.4 %reshape.40 = f32[28,2,4,1024]{3,2,1,0:T(4,128)S(1)} reshape(bf16[28,2,4096]{2,1,0:T(2,128)(2,1)} %param.6) | data formatting | bytes 1376256 | tf_op jit(solution)/shard_map/convert_element_type | solution.py:56
  21.7 0.0 copy-start.2
  21.7 0.0 copy-start.1
  21.7 0.5 fusion.12
  22.2 0.1 copy-done.2
  22.3 0.1 dynamic-slice
  22.4 0.5 copy-done.1
  22.9 0.1 dynamic-slice_add_fusion
  23.0 0.1 reshape.38
  23.1 0.0 copy-start.3
  23.1 0.2 copy.12
  23.3 0.6 multiply_reduce_fusion
  24.6 0.0 collective-permute-done
  24.6 0.0 collective-permute-done.1
  24.7 0.9 copy.13
  25.6 0.0 copy-done.3
  25.6 16.9 %fusion.7 = f32[1,224,256]{1,0,2:T(1,128)S(1)} fusion(bf16[1,8,1279]{1,0,2:T(2,128)(2,1)S(1)} %copy.13, s32[224]{0:T(256)S(1)} %copy-done.3, bf16[224,1024]{0,1:T(8,128)(2,1)S(1)} %copy.12), kind=kOutput, calls=%fused_computation.10 | convolution fusion | flops 943194112 | bytes 709488 | tf_op jit(solution)/shard_map/conv_general_dilated | solution.py:61
  42.5 0.1 copy.14
  42.7 0.1 fusion.13
  42.8 27.5 %all_gather.3 = bf16[28,64,256]{2,0,1:T(8,128)(2,1)S(1)} all-gather(bf16[28,4,256]{2,0,1:T(8,128)(2,1)S(1)} %fusion.13), channel_id=1, replica_groups=mesh['stn'=2,'vox'=16] {'vox'}, dimensions={1}, use_global_device_ids=true | all-gather | bytes 974848 | tf_op jit(solution)/shard_map/all_gather | solution.py:77
  70.4 0.5 copy.15
  70.9 28.9 %while.11 = (s32[]{:T(128)}, f32[64,4096]{1,0:T(8,128)S(1)}, bf16[28,64,256]{2,1,0:T(8,128)(2,1)S(1)}, s32[28,4096]{1,0:T(8,128)S(1)}, s32[]{:T(128)}, /*index=5*/s32[]{:T(128)}) while((s32[]{:T(128)}, f32[64,4096]{1,0:T(8,128)S(1)}, bf16[28,64,256]{2,1,0:T(8,128)(2,1)S(1)}, s32[28,4096]{1,0:T(8,128)S(1)}, s32[]{:T(128)}, ...), condition=%wide.region_4.5_spmd.clone, body=%wide.region_3.4_spmd.clone.sunk | while | flops 135790592 | bytes 2179159 | solution.py:92
  70.9 1.0 convolution_add_fusion.2
  72.0 1.0 convolution_add_fusion.2
  73.0 1.0 convolution_add_fusion.2
  74.0 1.0 convolution_add_fusion.2
  75.1 1.0 convolution_add_fusion.2
  76.1 1.0 convolution_add_fusion.2
  77.1 1.0 convolution_add_fusion.2
  78.1 1.0 convolution_add_fusion.2
  79.2 1.0 convolution_add_fusion.2
  80.2 1.0 convolution_add_fusion.2
  81.2 1.0 convolution_add_fusion.2
  82.3 1.0 convolution_add_fusion.2
  83.3 1.0 convolution_add_fusion.2
  84.3 1.0 convolution_add_fusion.2
  85.4 1.0 convolution_add_fusion.2
  86.4 1.0 convolution_add_fusion.2
  87.4 1.0 convolution_add_fusion.2
  88.5 1.0 convolution_add_fusion.2
  89.5 1.0 convolution_add_fusion.2
  90.5 1.0 convolution_add_fusion.2
  91.6 1.0 convolution_add_fusion.2
  92.6 1.0 convolution_add_fusion.2
  93.6 1.0 convolution_add_fusion.2
  94.7 1.0 convolution_add_fusion.2
  95.7 1.0 convolution_add_fusion.2
  96.7 1.0 convolution_add_fusion.2
  97.7 1.0 convolution_add_fusion.2
  98.8 1.0 convolution_add_fusion.2
  99.8 0.0 copy-start
  99.8 1.0 copy-done
  100.8 0.0 reduce-scatter.2.cloned.1.call-update
  100.8 16.8 %reduce-scatter.2.cloned.1.call-done = f32[32,4096]{1,0:T(8,128)} async-done(((f32[64,4096]{1,0:T(8,128)}), f32[32,4096]{1,0:T(8,128)}) %reduce-scatter.2.cloned.1.call-update) | async-done | bytes 524304 | tf_op jit(solution)/shard_map/reduce_scatter | solution.py:100
  117.6 1.9 %broadcast_multiply_fusion = f32[32,4096]{1,0:T(8,128)} fusion(f32[32,4096]{1,0:T(8,128)} %reduce-scatter.2.cloned.1.call-done), kind=kLoop, calls=%fused_computation.17 | loop fusion | flops 131072 | bytes 1048576 | tf_op jit(solution)/shard_map/mul | solution.py:101
  (40 shorter events, 0.7 us)
Async XLA Ops:
  6.5 111.1 %reduce-scatter.2.cloned.1.call-start = ((), (), s32[]{:S(2)}) async-start(), calls=%async_computation.1 | async-start | bytes 1572864 | tf_op jit(solution)/shard_map/reduce_scatter | solution.py:100
  17.6 6.9 %collective-permute-start = (bf16[2,128]{1,0:T(2,128)(2,1)S(1)}, bf16[2,128]{1,0:T(2,128)(2,1)S(1)}, u32[]{:S(2)}, u32[]{:S(2)}) collective-permute-start(bf16[2,128]{1,0:T(2,128)(2,1)S(1)} %get-tuple-element.64), channel_id=1, source_target_pairs={{0,1},{1,2},{2,3},{3,4},{4,5},{5,6},{6,7},{7,8},{8,9},{9,10},{10,1... | collective-permute-start | bytes 1544 | tf_op jit(solution)/shard_map/ppermute | solution.py:22
  18.9 5.6 %collective-permute-start.1 = (bf16[2,128]{1,0:T(2,128)(2,1)S(1)}, bf16[2,128]{1,0:T(2,128)(2,1)S(1)}, u32[]{:S(2)}, u32[]{:S(2)}) collective-permute-start(bf16[2,128]{1,0:T(2,128)(2,1)S(1)} %get-tuple-element.65), channel_id=1, source_target_pairs={{1,0},{2,1},{3,2},{4,3},{5,4},{6,5},{7,6},{8,7},{9,8},{10,9},{11,1... | collective-permute-start | bytes 1544 | tf_op jit(solution)/shard_map/ppermute | solution.py:25
  21.7 0.7 copy-start.2
  21.7 1.2 copy-start.1
  23.1 2.5 %copy-start.3 = (s32[224]{0:T(256)S(1)}, s32[224]{0:T(256)}, u32[]{:S(2)}) copy-start(s32[224]{0:T(256)} %constant.54.clone.1) | copy-start | bytes 2692
  99.8 1.0 copy-start
Sparse Core Ops, SparseCore 0:
  100.9 16.6 reduce-scatter.1
where the time goes:
time: 127 us; the launch traced here: 126 us
  matrix products  44.3 us (35%)
  blocking collectives  37.2 us (29%)
  waiting for transfers between devices  16.8 us (13%)
  between operations  14.9 us (12%)
  local copies, waits for them, and re-layouts  5.49 us (4%)
  other arithmetic  4.06 us (3%)
  starting transfers between devices  2.58 us (2%)
    all_gather x1, blocking collectives, shards(): corr_all = lax.all_gather(local_corr, 'vox', axis=1, tiled=True)  27.5 us
    dot_general x28, matrix products, add_station(): jnp.dot(corr_rows, selector, preferred_element_type=jnp.float32)  27.4 us
    conv_general_dilated x1, matrix products, shards(): lax.conv_general_dilated(segments, kernels, (1,), 'VALID', feature_group_...  16.9 us
    reduce_scatter x1, waiting for transfers between devices, shards(): lax.psum_scatter(running, 'stn', scatter_dimension=0, tiled=True)  16.8 us
    psum x1, blocking collectives, spread(): return lax.psum(kept, axis)  9.65 us
  transfers between devices with their start and end apart: 3, of which 1 were waited for; matrix products, arithmetic and copies ran while one was open for 2% of the time, Pallas kernels for 0%

commit v1 on v0

--- a/solution.py
+++ b/solution.py
@@ -11,7 +11,7 @@
 
 def spread(value, axis, source):
     kept = jnp.where(lax.axis_index(axis) == source, value, 0).astype(value.dtype)
-    return lax.psum(kept, axis)
+    return jnp.sum(lax.all_gather(kept, axis), axis=0)
 
 
 def padded(block, sides, width):

time: 127 us -> 124 us (0.976)
  blocking collectives: 37.2 us -> 33.5 us
    psum x1 -> x0, blocking collectives: 9.65 us -> none  [spread(): return lax.psum(kept, axis)]
    all_gather x0 -> x1, blocking collectives: none -> 5.31 us  [spread(): return jnp.sum(lax.all_gather(kept, axis), axis=0)]
  transfers between devices with their start and end apart: 3 -> 3, of which waited for: 1 -> 1; matrix products, arithmetic and copies ran while one was open for 2% -> 3% of each run, Pallas kernels for 0% -> 0%
where the time goes in v1:
time: 124 us; the launch traced here: 123 us
  matrix products  44.2 us (36%)
  blocking collectives  33.5 us (27%)
  waiting for transfers between devices  17.8 us (14%)
  between operations  14.9 us (12%)
  local copies, waits for them, and re-layouts  5.31 us (4%)
  other arithmetic  4.1 us (3%)
  starting transfers between devices  2.58 us (2%)
    all_gather x1, blocking collectives, shards(): corr_all = lax.all_gather(local_corr, 'vox', axis=1, tiled=True)  28.2 us
    dot_general x28, matrix products, add_station(): jnp.dot(corr_rows, selector, preferred_element_type=jnp.float32)  27.4 us
    reduce_scatter x1, waiting for transfers between devices, shards(): lax.psum_scatter(running, 'stn', scatter_dimension=0, tiled=True)  17.8 us
    conv_general_dilated x1, matrix products, shards(): lax.conv_general_dilated(segments, kernels, (1,), 'VALID', feature_group_...  16.9 us
    all_gather x1, blocking collectives, spread(): return jnp.sum(lax.all_gather(kept, axis), axis=0)  5.31 us
  transfers between devices with their start and end apart: 3, of which 1 were waited for; matrix products, arithmetic and copies ran while one was open for 3% of the time, Pallas kernels for 0%

profile of v1, /device:TPU:0, one launch (start us, length us, event | category | flops | bytes accessed | tf_op | source)
XLA Modules:
  0.0 123.4 jit_solution(9715656799755949595)
XLA Ops:
  6.5 0.0 reduce-scatter.2.cloned.1.call-start
  7.2 0.7 broadcast_select_fusion
  8.0 5.3 %all_gather.7 = bf16[2,2,4096]{2,1,0:T(2,128)(2,1)S(1)} all-gather(bf16[1,2,4096]{2,1,0:T(2,128)(2,1)S(1)} %broadcast_select_fusion), channel_id=1, replica_groups=mesh['stn'=2,'vox'=16] {'stn'}, dimensions={0}, use_global_device_ids=true | all-gather | bytes 49152 | tf_op jit(solution)/shard_map/all_gather | solution.py:14
  13.3 1.3 %collective-permute-start = (bf16[2,128]{1,0:T(2,128)(2,1)S(1)}, bf16[2,128]{1,0:T(2,128)(2,1)S(1)}, u32[]{:S(2)}, u32[]{:S(2)}) collective-permute-start(bf16[2,128]{1,0:T(2,128)(2,1)S(1)} %get-tuple-element.64), channel_id=1, source_target_pairs={{0,1},{1,2},{2,3},{3,4},{4,5},{5,6},{6,7},{7,8},{8,9},{9,10},{10,1... | collective-permute-start | bytes 1544 | tf_op jit(solution)/shard_map/ppermute | solution.py:22
  14.6 1.3 %collective-permute-start.1 = (bf16[2,128]{1,0:T(2,128)(2,1)S(1)}, bf16[2,128]{1,0:T(2,128)(2,1)S(1)}, u32[]{:S(2)}, u32[]{:S(2)}) collective-permute-start(bf16[2,128]{1,0:T(2,128)(2,1)S(1)} %get-tuple-element.65), channel_id=1, source_target_pairs={{1,0},{2,1},{3,2},{4,3},{5,4},{6,5},{7,6},{8,7},{9,8},{10,9},{11,1... | collective-permute-start | bytes 1544 | tf_op jit(solution)/shard_map/ppermute | solution.py:25
  15.9 1.4 %reshape.37 = f32[28,2,4,1024]{3,2,1,0:T(4,128)S(1)} reshape(bf16[28,2,4096]{2,1,0:T(2,128)(2,1)} %param.6) | data formatting | bytes 1376256 | tf_op jit(solution)/shard_map/convert_element_type | solution.py:56
  17.4 0.0 copy-start.2
  17.4 0.0 copy-start.1
  17.4 0.5 fusion.12
  17.9 0.1 copy-done.2
  18.0 0.1 dynamic-slice
  18.1 0.5 copy-done.1
  18.6 0.1 dynamic-slice_add_fusion
  18.7 0.1 reshape.35
  18.8 0.0 copy-start.3
  18.8 0.2 copy.11
  19.0 0.6 multiply_reduce_fusion
  20.3 0.0 collective-permute-done
  20.3 0.0 collective-permute-done.1
  20.4 0.7 copy.12
  21.1 0.0 copy-done.3
  21.1 16.9 %fusion.7 = f32[1,224,256]{1,0,2:T(1,128)S(1)} fusion(bf16[1,8,1279]{1,0,2:T(2,128)(2,1)S(1)} %copy.12, s32[224]{0:T(256)S(1)} %copy-done.3, bf16[224,1024]{0,1:T(8,128)(2,1)S(1)} %copy.11), kind=kOutput, calls=%fused_computation.10 | convolution fusion | flops 943194112 | bytes 709488 | tf_op jit(solution)/shard_map/conv_general_dilated | solution.py:61
  38.0 0.1 copy.13
  38.2 0.1 fusion.13
  38.3 28.2 %all_gather.8 = bf16[28,64,256]{2,0,1:T(8,128)(2,1)S(1)} all-gather(bf16[28,4,256]{2,0,1:T(8,128)(2,1)S(1)} %fusion.13), channel_id=1, replica_groups=mesh['stn'=2,'vox'=16] {'vox'}, dimensions={1}, use_global_device_ids=true | all-gather | bytes 974848 | tf_op jit(solution)/shard_map/all_gather | solution.py:77
  66.5 0.5 copy.14
  67.0 28.9 %while.11 = (s32[]{:T(128)}, f32[64,4096]{1,0:T(8,128)S(1)}, bf16[28,64,256]{2,1,0:T(8,128)(2,1)S(1)}, s32[28,4096]{1,0:T(8,128)S(1)}, s32[]{:T(128)}, /*index=5*/s32[]{:T(128)}) while((s32[]{:T(128)}, f32[64,4096]{1,0:T(8,128)S(1)}, bf16[28,64,256]{2,1,0:T(8,128)(2,1)S(1)}, s32[28,4096]{1,0:T(8,128)S(1)}, s32[]{:T(128)}, ...), condition=%wide.region_4.5_spmd.clone, body=%wide.region_3.4_spmd.clone.sunk | while | flops 135790592 | bytes 2179159 | solution.py:92
  67.0 1.0 convolution_add_fusion.2
  68.0 1.0 convolution_add_fusion.2
  69.1 1.0 convolution_add_fusion.2
  70.1 1.0 convolution_add_fusion.2
  71.1 1.0 convolution_add_fusion.2
  72.2 1.0 convolution_add_fusion.2
  73.2 1.0 convolution_add_fusion.2
  74.2 1.0 convolution_add_fusion.2
  75.3 1.0 convolution_add_fusion.2
  76.3 1.0 convolution_add_fusion.2
  77.3 1.0 convolution_add_fusion.2
  78.4 1.0 convolution_add_fusion.2
  79.4 1.0 convolution_add_fusion.2
  80.4 1.0 convolution_add_fusion.2
  81.5 1.0 convolution_add_fusion.2
  82.5 1.0 convolution_add_fusion.2
  83.5 1.0 convolution_add_fusion.2
  84.6 1.0 convolution_add_fusion.2
  85.6 1.0 convolution_add_fusion.2
  86.6 1.0 convolution_add_fusion.2
  87.6 1.0 convolution_add_fusion.2
  88.7 1.0 convolution_add_fusion.2
  89.7 1.0 convolution_add_fusion.2
  90.7 1.0 convolution_add_fusion.2
  91.8 1.0 convolution_add_fusion.2
  92.8 1.0 convolution_add_fusion.2
  93.8 1.0 convolution_add_fusion.2
  94.9 1.0 convolution_add_fusion.2
  95.9 0.0 copy-start
  95.9 1.0 copy-done
  96.9 0.0 reduce-scatter.2.cloned.1.call-update
  96.9 17.8 %reduce-scatter.2.cloned.1.call-done = f32[32,4096]{1,0:T(8,128)} async-done(((f32[64,4096]{1,0:T(8,128)}), f32[32,4096]{1,0:T(8,128)}) %reduce-scatter.2.cloned.1.call-update) | async-done | bytes 524304 | tf_op jit(solution)/shard_map/reduce_scatter | solution.py:100
  114.6 1.9 %broadcast_multiply_fusion = f32[32,4096]{1,0:T(8,128)} fusion(f32[32,4096]{1,0:T(8,128)} %reduce-scatter.2.cloned.1.call-done), kind=kLoop, calls=%fused_computation.17 | loop fusion | flops 131072 | bytes 1048576 | tf_op jit(solution)/shard_map/mul | solution.py:101
  (41 shorter events, 0.8 us)
Async XLA Ops:
  6.5 108.1 %reduce-scatter.2.cloned.1.call-start = ((), (), s32[]{:S(2)}) async-start(), calls=%async_computation.1 | async-start | bytes 1572864 | tf_op jit(solution)/shard_map/reduce_scatter | solution.py:100
  13.3 6.9 %collective-permute-start = (bf16[2,128]{1,0:T(2,128)(2,1)S(1)}, bf16[2,128]{1,0:T(2,128)(2,1)S(1)}, u32[]{:S(2)}, u32[]{:S(2)}) collective-permute-start(bf16[2,128]{1,0:T(2,128)(2,1)S(1)} %get-tuple-element.64), channel_id=1, source_target_pairs={{0,1},{1,2},{2,3},{3,4},{4,5},{5,6},{6,7},{7,8},{8,9},{9,10},{10,1... | collective-permute-start | bytes 1544 | tf_op jit(solution)/shard_map/ppermute | solution.py:22
  14.6 5.6 %collective-permute-start.1 = (bf16[2,128]{1,0:T(2,128)(2,1)S(1)}, bf16[2,128]{1,0:T(2,128)(2,1)S(1)}, u32[]{:S(2)}, u32[]{:S(2)}) collective-permute-start(bf16[2,128]{1,0:T(2,128)(2,1)S(1)} %get-tuple-element.65), channel_id=1, source_target_pairs={{1,0},{2,1},{3,2},{4,3},{5,4},{6,5},{7,6},{8,7},{9,8},{10,9},{11,1... | collective-permute-start | bytes 1544 | tf_op jit(solution)/shard_map/ppermute | solution.py:25
  17.4 0.7 copy-start.2
  17.4 1.2 copy-start.1
  18.8 2.3 %copy-start.3 = (s32[224]{0:T(256)S(1)}, s32[224]{0:T(256)}, u32[]{:S(2)}) copy-start(s32[224]{0:T(256)} %constant.55.clone.1) | copy-start | bytes 2692
  95.9 1.0 copy-start
Sparse Core Ops, SparseCore 0:
  97.0 17.5 reduce-scatter.1
